TPU v7x, 512 devices: a whole 4x4x16 slice. The times are simulated.
512 devices in a mesh: sec: 16 (over z_lo, y), tile: 32 (over x, z_hi, core).
Axes of the slice: x: 4, y: 4, z: 16 (z_hi: 4, z_lo: 4; z = z_hi * 4 + z_lo), core: 2. Of those that a mesh axis runs over, the one named last changes fastest.
Arguments:
- snapshots: bfloat16 [5, 256, 3072, 256], P(None, 'sec', 'tile'), may hold values from -6 to 6
- eig_columns: bfloat16 [256, 256], P(None, 'tile'), may hold values from -0.375 to 0.375
- mean_u: float32 [256, 3072], P('sec', 'tile'), may hold values from 0.2 to 1
- mean_v: float32 [256, 3072], P('sec', 'tile'), may hold values from -0.5 to 0.5
- mean_rho: float32 [256, 3072], P('sec', 'tile'), may hold values from 0.5 to 2
- mean_shear: float32 [256, 3072], P('sec', 'tile'), may hold values from 0.2 to 2
- sound: float32 [256, 3072], P('sec', 'tile'), may hold values from 0.5 to 4
Outputs:
- rayleigh: float32 [16, 256, 256], P('sec', 'tile')
All inputs are finite; a program needn't handle non-finite values.
Results may differ from a plain program's by a relative error of at most 0.0044.
Values may be sent and summed in bfloat16 or wider, within the bound.
No kernel may reach another device: no remote copies, remote signals or barrier semaphores. Data moves between devices by JAX's collectives and lax.ppermute only.
A program may use at most 64 MiB of HBM per device.

v0:
```python
import jax
import jax.numpy as jnp
from jax import lax
from jax.sharding import PartitionSpec as P

viscosity = 0.002


def extended(cells, sides, width):
    for axis, dim in sides:
        count = lax.axis_size(axis)
        ends = count - 1
        head = lax.slice_in_dim(cells, 0, width, axis=dim)
        tail = lax.slice_in_dim(cells, cells.shape[dim] - width, cells.shape[dim], axis=dim)
        cells = jnp.concatenate(
            [
                lax.ppermute(tail, axis, [(i, (i + 1) % count) for i in range(ends)]),
                cells,
                lax.ppermute(head, axis, [((i + 1) % count, i) for i in range(ends)]),
            ],
            axis=dim,
        )
    return cells


def prefix(value, axis, join, neutral):
    count, mine = (lax.axis_size(axis), lax.axis_index(axis))
    pieces = lax.all_gather(value, axis)
    subtotal = jnp.full_like(value, 0) + jnp.asarray(neutral, value.dtype)

    def lap(position, subtotal):
        longer = join(subtotal, pieces[position])
        return jnp.where(position < mine, longer, subtotal)

    return lax.fori_loop(0, count - 1, lap, subtotal)


def field_at(padded, k, off_x, off_y):
    end_x = padded.shape[1] - 1 + off_x
    end_y = padded.shape[2] - 1 + off_y
    return padded[k, 1 + off_x : end_x, 1 + off_y : end_y, :].astype(jnp.float32)


def gradient(padded, k):
    along_x = (field_at(padded, k, 1, 0) - field_at(padded, k, -1, 0)) * 0.5
    along_y = (field_at(padded, k, 0, 1) - field_at(padded, k, 0, -1)) * 0.5
    return (along_x, along_y)


def laplace(padded, k):
    total = field_at(padded, k, 1, 0) + field_at(padded, k, -1, 0)
    total = total + field_at(padded, k, 0, 1) + field_at(padded, k, 0, -1)
    return total - 4.0 * field_at(padded, k, 0, 0)


def stencil(padded, mean_u, mean_v, mean_rho, mean_shear, sound):
    flow_x = mean_u[:, :, None]
    flow_y = mean_v[:, :, None]
    density = mean_rho[:, :, None]
    inverse = 1.0 / density
    shear = mean_shear[:, :, None]
    stiff = sound[:, :, None]
    rho_x, rho_y = gradient(padded, 0)
    u_x, u_y = gradient(padded, 1)
    v_x, v_y = gradient(padded, 2)
    w_x, w_y = gradient(padded, 3)
    p_x, p_y = gradient(padded, 4)
    diverge = u_x + v_y
    image_rho = -(flow_x * rho_x + flow_y * rho_y) - density * diverge
    image_u = (
        -(flow_x * u_x + flow_y * u_y)
        - shear * field_at(padded, 2, 0, 0)
        - inverse * p_x
        + viscosity * laplace(padded, 1)
    )
    image_v = -(flow_x * v_x + flow_y * v_y) - inverse * p_y + viscosity * laplace(padded, 2)
    image_w = -(flow_x * w_x + flow_y * w_y) + viscosity * laplace(padded, 3)
    image_p = -(flow_x * p_x + flow_y * p_y) - stiff * diverge
    return jnp.stack([image_rho, image_u, image_v, image_w, image_p]).astype(jnp.bfloat16)


def form_modes(block, piece):
    return jnp.einsum("fxys,sk->fxyk", block, piece, preferred_element_type=jnp.float32).astype(
        jnp.bfloat16
    )


def add_blocks(earlier, later):
    return earlier + later


def body(snapshots, eig_columns, mean_u, mean_v, mean_rho, mean_shear, sound):
    sections = lax.axis_size("sec")
    tiles_n = lax.axis_size("tile")
    cells_x = snapshots.shape[1]
    cells_y = snapshots.shape[2]
    scale = float(5 * cells_x * cells_y * sections * tiles_n) ** (-0.5)
    modes = form_modes(snapshots, lax.all_gather(eig_columns, "tile", axis=1, tiled=True))
    padded = extended(modes, (("sec", 1), ("tile", 2)), 1)
    image = stencil(padded, mean_u, mean_v, mean_rho, mean_shear, sound)
    own_rows = lax.psum_scatter(
        jnp.einsum("fxyk,fxyl->kl", modes, image, preferred_element_type=jnp.float32) * scale,
        "tile",
        scatter_dimension=0,
        tiled=True,
    )
    upstream = prefix(own_rows, "sec", add_blocks, jnp.zeros_like(own_rows))
    prefix_sum = upstream + own_rows
    return prefix_sum[None]


def solution(mesh):
    in_specs = (
        P(None, "sec", "tile", None),
        P(None, "tile"),
        P("sec", "tile"),
        P("sec", "tile"),
        P("sec", "tile"),
        P("sec", "tile"),
        P("sec", "tile"),
    )
    out_specs = P("sec", "tile", None)
    return jax.shard_map(body, mesh=mesh, in_specs=in_specs, out_specs=out_specs, check_vma=False)
```

profile of v0, /device:TPU:2, one launch (start us, length us, event | category | flops | bytes accessed | tf_op | source)
XLA Modules:
  0.0 275.3 jit_solution(12448692880432046577)
XLA Ops:
  6.5 0.0 reduce-scatter.2.cloned.1.call-start
  6.5 55.4 %all_gather.9 = bf16[256,256]{0,1:T(8,128)(2,1)S(1)} all-gather(bf16[256,8]{0,1:T(8,128)(2,1)} %param.10), channel_id=1, replica_groups=mesh['sec'=16,'tile'=32] {'tile'}, dimensions={1}, use_global_device_ids=true | all-gather | bytes 135168 | tf_op jit(solution)/shard_map/all_gather | solution.py:98
  61.9 0.0 copy-start.1
  61.9 0.0 copy-start.2
  61.9 3.4 %convolution_convert_fusion = bf16[5,16,96,256]{3,2,1,0:T(8,128)(2,1)S(1)} fusion(bf16[5,16,96,256]{3,2,1,0:T(8,128)(2,1)} %param.9, bf16[256,256]{0,1:T(8,128)(2,1)S(1)} %all_gather.9), kind=kOutput, calls=%fused_computation.1 | convolution fusion | flops 1008599040 | bytes 7995392 | tf_op jit(solution)/shard_map/fxys,sk->fxyk/dot_general | solution.py:83
  65.3 1.3 collective-permute-start
  66.6 4.6 %collective-permute-start.1 = (bf16[5,1,96,256]{3,2,1,0:T(8,128)(2,1)S(1)}, bf16[5,1,96,256]{3,2,1,0:T(8,128)(2,1)S(1)}, u32[]{:S(2)}, u32[]{:S(2)}) collective-permute-start(bf16[5,1,96,256]{3,2,1,0:T(8,128)(2,1)S(1)} %get-tuple-element.110), channel_id=1, source_target_pairs={{0,32},{32,64},{64,96},{96,128},{128,160},{160,192},{192,224},{224... | collective-permute-start | bytes 737288 | tf_op jit(solution)/shard_map/ppermute | solution.py:17
  71.2 0.0 copy-done.1
  71.2 0.0 copy-done.2
  71.2 0.0 copy-start.3
  71.2 0.0 copy-start.4
  71.2 4.2 %collective-permute-done = bf16[5,1,96,256]{3,2,1,0:T(8,128)(2,1)S(1)} collective-permute-done((bf16[5,1,96,256]{3,2,1,0:T(8,128)(2,1)S(1)}, bf16[5,1,96,256]{3,2,1,0:T(8,128)(2,1)S(1)}, u32[]{:S(2)}, u32[]{:S(2)}) %collective-permute-start) | collective-permute-done | bytes 245792 | tf_op jit(solution)/shard_map/ppermute | solution.py:19
  75.4 1.2 collective-permute-done.1
  76.6 0.1 pad_maximum_fusion.18
  76.7 4.2 %collective-permute-start.2 = (bf16[5,18,1,256]{3,2,1,0:T(2,128)(2,1)S(1)}, bf16[5,18,1,256]{3,2,1,0:T(2,128)(2,1)S(1)}, u32[]{:S(2)}, u32[]{:S(2)}) collective-permute-start(bf16[5,18,1,256]{3,2,1,0:T(2,128)(2,1)S(1)} %get-tuple-element.108), channel_id=1, source_target_pairs={{1,0},{2,1},{3,2},{4,3},{5,4},{6,5},{7,6},{8,7},{9,8},{10,9},{11,1... | collective-permute-start | bytes 138248 | tf_op jit(solution)/shard_map/ppermute | solution.py:19
  80.9 1.9 collective-permute-start.3
  82.9 0.0 copy-done.3
  82.9 0.0 copy-done.4
  82.9 0.2 collective-permute-done.2
  83.1 8.5 %collective-permute-done.3 = bf16[5,18,1,256]{3,2,1,0:T(2,128)(2,1)S(1)} collective-permute-done((bf16[5,18,1,256]{3,2,1,0:T(2,128)(2,1)S(1)}, bf16[5,18,1,256]{3,2,1,0:T(2,128)(2,1)S(1)}, u32[]{:S(2)}, u32[]{:S(2)}) %collective-permute-start.3) | collective-permute-done | bytes 46112 | tf_op jit(solution)/shard_map/ppermute | solution.py:17
  91.6 0.0 copy-start
  91.6 5.0 %fusion.27 = bf16[5,16,96,256]{3,2,1,0:T(8,128)(2,1)S(1)} fusion(bf16[5,18,1,256]{3,2,1,0:T(2,128)(2,1)S(1)} %collective-permute-done.3, bf16[5,1,96,256]{3,2,1,0:T(8,128)(2,1)S(1)} %collective-permute-done, bf16[5,16,96,256]{3,2,1,0:T(8,128)(2,1)S(1)} %convolution_convert_fusion, bf16[5,1,96,256]{3,2,1,0:T(8,128)(2,1)S(1)} %collective-permute-done.1, ...), kind=kLoop, calls=%fused_computation.51 | loop fusion | flops 23592960 | bytes 5320704
  96.6 0.0 copy-done
  96.6 2.6 fusion.30
  99.2 5.2 %fusion.31 = bf16[5,16,96,256]{3,2,1,0:T(8,128)(2,1)S(1)} fusion(bf16[5,16,96,256]{3,2,1,0:T(8,128)(2,1)S(1)} %fusion.30, bf16[5,16,96,256]{3,2,1,0:T(8,128)(2,1)S(1)} %convolution_convert_fusion, bf16[5,1,96,256]{3,2,1,0:T(8,128)(2,1)S(1)} %collective-permute-done.1, bf16[5,1,96,256]{3,2,1,0:T(8,128)(2,1)S(1)} %collective-permute-done, ...), kind=kLoop, calls=%fused_computation.55 | loop fusion | flops 22806528 | bytes 6205440
  104.5 2.1 fusion.29
  106.6 5.7 %fusion.28 = bf16[5,16,96,256]{3,2,1,0:T(8,128)(2,1)S(1)} fusion(bf16[5,16,96,256]{3,2,1,0:T(8,128)(2,1)S(1)} %fusion.29, f32[16,96]{1,0:T(8,128)S(1)} %get-tuple-element.115, f32[16,96]{1,0:T(8,128)S(1)} %get-tuple-element.114, f32[16,96]{1,0:T(8,128)S(1)} %get-tuple-element.116, bf16[5,1,96,256]{3,2,1,0:T(8,128)(2,1)S(1)} %collective-permute-done, ...), kind=kLoop, calls=%fused_computation.52 | loop fusion | flops 23592960 | bytes 5419008 | tf_op jit(solution)/shard_map/stack | solution.py:79
  112.3 1.9 fusion.26
  114.2 0.0 reduce-scatter.2.cloned.1.call-update
  114.3 110.3 %reduce-scatter.2.cloned.1.call-done = f32[8,256]{1,0:T(8,128)} async-done(((f32[256,256]{1,0:T(8,128)}), f32[8,256]{1,0:T(8,128)}) %reduce-scatter.2.cloned.1.call-update) | async-done | bytes 8208 | tf_op jit(solution)/shard_map/reduce_scatter | solution.py:101
  224.6 42.1 %all-gather = f32[128,256]{1,0:T(8,128)S(1)} all-gather(f32[8,256]{1,0:T(8,128)} %reduce-scatter.2.cloned.1.call-done), channel_id=2, replica_groups=mesh['sec'=16,'tile'=32] {'sec'}, dimensions={0}, use_global_device_ids=true | all-gather | bytes 139264 | tf_op jit(solution)/shard_map/all_gather | solution.py:28
  266.7 0.5 while.14
  267.2 1.3 add_bitcast_fusion
  (19 shorter events, 0.2 us)
Async XLA Ops:
  6.5 218.1 %reduce-scatter.2.cloned.1.call-start = ((), (), s32[]{:S(2)}) async-start(), calls=%async_computation.1 | async-start | bytes 270336 | tf_op jit(solution)/shard_map/reduce_scatter | solution.py:101
  61.9 9.3 %copy-start.1 = (f32[16,96]{1,0:T(8,128)S(1)}, f32[16,96]{1,0:T(8,128)}, u32[]{:S(2)}) copy-start(f32[16,96]{1,0:T(8,128)} %param.13) | copy-start | bytes 18436
  61.9 9.3 %copy-start.2 = (f32[16,96]{1,0:T(8,128)S(1)}, f32[16,96]{1,0:T(8,128)}, u32[]{:S(2)}) copy-start(f32[16,96]{1,0:T(8,128)} %param.12) | copy-start | bytes 18436
  65.3 10.1 %collective-permute-start = (bf16[5,1,96,256]{3,2,1,0:T(8,128)(2,1)S(1)}, bf16[5,1,96,256]{3,2,1,0:T(8,128)(2,1)S(1)}, u32[]{:S(2)}, u32[]{:S(2)}) collective-permute-start(bf16[5,1,96,256]{3,2,1,0:T(8,128)(2,1)S(1)} %get-tuple-element.111), channel_id=1, source_target_pairs={{32,0},{64,32},{96,64},{128,96},{160,128},{192,160},{224,192},{256... | collective-permute-start | bytes 737288 | tf_op jit(solution)/shard_map/ppermute | solution.py:19
  66.6 10.0 %collective-permute-start.1 = (bf16[5,1,96,256]{3,2,1,0:T(8,128)(2,1)S(1)}, bf16[5,1,96,256]{3,2,1,0:T(8,128)(2,1)S(1)}, u32[]{:S(2)}, u32[]{:S(2)}) collective-permute-start(bf16[5,1,96,256]{3,2,1,0:T(8,128)(2,1)S(1)} %get-tuple-element.110), channel_id=1, source_target_pairs={{0,32},{32,64},{64,96},{96,128},{128,160},{160,192},{192,224},{224... | collective-permute-start | bytes 737288 | tf_op jit(solution)/shard_map/ppermute | solution.py:17
  71.2 11.7 %copy-start.3 = (f32[16,96]{1,0:T(8,128)S(1)}, f32[16,96]{1,0:T(8,128)}, u32[]{:S(2)}) copy-start(f32[16,96]{1,0:T(8,128)} %param.15) | copy-start | bytes 18436
  71.2 11.7 %copy-start.4 = (f32[16,96]{1,0:T(8,128)S(1)}, f32[16,96]{1,0:T(8,128)}, u32[]{:S(2)}) copy-start(f32[16,96]{1,0:T(8,128)} %param.11) | copy-start | bytes 18436
  76.7 6.3 %collective-permute-start.2 = (bf16[5,18,1,256]{3,2,1,0:T(2,128)(2,1)S(1)}, bf16[5,18,1,256]{3,2,1,0:T(2,128)(2,1)S(1)}, u32[]{:S(2)}, u32[]{:S(2)}) collective-permute-start(bf16[5,18,1,256]{3,2,1,0:T(2,128)(2,1)S(1)} %get-tuple-element.108), channel_id=1, source_target_pairs={{1,0},{2,1},{3,2},{4,3},{5,4},{6,5},{7,6},{8,7},{9,8},{10,9},{11,1... | collective-permute-start | bytes 138248 | tf_op jit(solution)/shard_map/ppermute | solution.py:19
  80.9 10.7 %collective-permute-start.3 = (bf16[5,18,1,256]{3,2,1,0:T(2,128)(2,1)S(1)}, bf16[5,18,1,256]{3,2,1,0:T(2,128)(2,1)S(1)}, u32[]{:S(2)}, u32[]{:S(2)}) collective-permute-start(bf16[5,18,1,256]{3,2,1,0:T(2,128)(2,1)S(1)} %get-tuple-element.109), channel_id=1, source_target_pairs={{0,1},{1,2},{2,3},{3,4},{4,5},{5,6},{6,7},{7,8},{8,9},{9,10},{10,1... | collective-permute-start | bytes 138248 | tf_op jit(solution)/shard_map/ppermute | solution.py:17
  91.6 5.0 %copy-start = (f32[16,96]{1,0:T(8,128)S(1)}, f32[16,96]{1,0:T(8,128)}, u32[]{:S(2)}) copy-start(f32[16,96]{1,0:T(8,128)} %param.14) | copy-start | bytes 18436
Sparse Core Ops, SparseCore 0:
  114.4 110.1 reduce-scatter.1
where the time goes:
time: 276 us; the launch traced here: 275 us
  waiting for transfers between devices  124 us (45%)
  blocking collectives  97.4 us (35%)
  other arithmetic  22.2 us (8%)
  between operations  13.6 us (5%)
  starting transfers between devices  12 us (4%)
  matrix products  5.3 us (2%)
    reduce_scatter x1, waiting for transfers between devices, body(): lax.psum_scatter(jnp.einsum('fxyk,fxyl->kl', modes, image, preferred_elem...  110 us
    all_gather x1, blocking collectives, body(): lax.all_gather(eig_columns, 'tile', axis=1, tiled=True)  55.4 us
    all_gather x1, blocking collectives, prefix(): pieces = lax.all_gather(value, axis)  42.1 us
    unnamed x5, other arithmetic  14.9 us
    ppermute x2, waiting for transfers between devices, extended(): lax.ppermute(tail, axis, [(i, (i + 1) % count) for i in range(ends)])  9.72 us
    ppermute x2, starting transfers between devices, extended(): lax.ppermute(tail, axis, [(i, (i + 1) % count) for i in range(ends)])  6.48 us
    another operation x1, other arithmetic, stencil(): jnp.stack([image_rho, image_u, image_v, image_w, image_p])  5.68 us
  transfers between devices with their start and end apart: 5, of which 5 were waited for; matrix products, arithmetic and copies ran while one was open for 0% of the time, Pallas kernels for 0%

commit v1 on v0

--- a/solution.py
+++ b/solution.py
@@ -4,6 +4,11 @@
 from jax.sharding import PartitionSpec as P
 
 viscosity = 0.002
+
+
+def exchange_gather(shard, axis, dim):
+    sent = jnp.stack([shard] * lax.axis_size(axis))
+    return jnp.concatenate(lax.all_to_all(sent, axis, 0, 0), axis=dim)
 
 
 def extended(cells, sides, width):
@@ -95,7 +100,7 @@
     cells_x = snapshots.shape[1]
     cells_y = snapshots.shape[2]
     scale = float(5 * cells_x * cells_y * sections * tiles_n) ** (-0.5)
-    modes = form_modes(snapshots, lax.all_gather(eig_columns, "tile", axis=1, tiled=True))
+    modes = form_modes(snapshots, exchange_gather(eig_columns, "tile", 1))
     padded = extended(modes, (("sec", 1), ("tile", 2)), 1)
     image = stencil(padded, mean_u, mean_v, mean_rho, mean_shear, sound)
     own_rows = lax.psum_scatter(

time: 276 us -> 254 us (0.920)
  blocking collectives: 97.4 us -> 74.5 us
    all_gather x1 -> x0, blocking collectives: 55.4 us -> none  [body(): lax.all_gather(eig_columns, 'tile', axis=1, tiled=True)]
    all_to_all x0 -> x1, blocking collectives: none -> 32.4 us  [exchange_gather(): return jnp.concatenate(lax.all_to_all(sent, axis, 0, 0), axis=dim)]
where the time goes in v1:
time: 254 us
  waiting for transfers between devices  126 us (50%)
  blocking collectives  74.5 us (29%)
  other arithmetic  22.2 us (9%)
  between operations  13.6 us (5%)
  starting transfers between devices  10.7 us (4%)
  matrix products  5.3 us (2%)
    reduce_scatter x1, waiting for transfers between devices, body(): lax.psum_scatter(jnp.einsum('fxyk,fxyl->kl', modes, image, preferred_elem...  112 us
    all_gather x1, blocking collectives, prefix(): pieces = lax.all_gather(value, axis)  42.1 us
    all_to_all x1, blocking collectives, exchange_gather(): return jnp.concatenate(lax.all_to_all(sent, axis, 0, 0), axis=dim)  32.4 us
    unnamed x5, other arithmetic  14.9 us
    ppermute x2, waiting for transfers between devices, extended(): lax.ppermute(tail, axis, [(i, (i + 1) % count) for i in range(ends)])  10.3 us
    ppermute x2, starting transfers between devices, extended(): lax.ppermute(tail, axis, [(i, (i + 1) % count) for i in range(ends)])  6.48 us
    another operation x1, other arithmetic, stencil(): jnp.stack([image_rho, image_u, image_v, image_w, image_p])  5.68 us
  transfers between devices with their start and end apart: 5, of which 5 were waited for; matrix products, arithmetic and copies ran while one was open for 0% of the time, Pallas kernels for 0%

profile of v1, /device:TPU:2, one launch (start us, length us, event | category | flops | bytes accessed | tf_op | source)
XLA Modules:
  0.0 253.7 jit_solution(12426162331017223167)
XLA Ops:
  6.5 0.0 reduce-scatter.2.cloned.1.call-start
  6.5 0.7 stack.5
  7.2 32.4 %all_to_all.5 = bf16[32,256,8]{1,2,0:T(8,128)(2,1)S(1)} all-to-all(bf16[32,256,8]{1,2,0:T(8,128)(2,1)S(1)} %stack.5), channel_id=1, replica_groups=mesh['sec'=16,'tile'=32] {'tile'}, dimensions={0} | all-to-all | bytes 262144 | tf_op jit(solution)/shard_map/all_to_all | solution.py:11
  39.6 0.0 copy-start.1
  39.6 0.0 copy-start.2
  39.6 3.4 %convolution_convert_fusion = bf16[5,16,96,256]{3,2,1,0:T(8,128)(2,1)S(1)} fusion(bf16[5,16,96,256]{3,2,1,0:T(8,128)(2,1)} %param.9, bf16[32,256,8]{1,2,0:T(8,128)(2,1)S(1)} %all_to_all.5), kind=kOutput, calls=%fused_computation.1 | convolution fusion | flops 1008599040 | bytes 7995392 | tf_op jit(solution)/shard_map/fxys,sk->fxyk/dot_general | solution.py:88
  43.0 1.3 collective-permute-start
  44.3 4.6 %collective-permute-start.1 = (bf16[5,1,96,256]{3,2,1,0:T(8,128)(2,1)S(1)}, bf16[5,1,96,256]{3,2,1,0:T(8,128)(2,1)S(1)}, u32[]{:S(2)}, u32[]{:S(2)}) collective-permute-start(bf16[5,1,96,256]{3,2,1,0:T(8,128)(2,1)S(1)} %get-tuple-element.110), channel_id=1, source_target_pairs={{0,32},{32,64},{64,96},{96,128},{128,160},{160,192},{192,224},{224... | collective-permute-start | bytes 737288 | tf_op jit(solution)/shard_map/ppermute | solution.py:22
  48.9 0.0 copy-done.1
  48.9 0.0 copy-done.2
  49.0 0.0 copy-start.3
  49.0 0.0 copy-start.4
  49.0 4.1 %collective-permute-done = bf16[5,1,96,256]{3,2,1,0:T(8,128)(2,1)S(1)} collective-permute-done((bf16[5,1,96,256]{3,2,1,0:T(8,128)(2,1)S(1)}, bf16[5,1,96,256]{3,2,1,0:T(8,128)(2,1)S(1)}, u32[]{:S(2)}, u32[]{:S(2)}) %collective-permute-start) | collective-permute-done | bytes 245792 | tf_op jit(solution)/shard_map/ppermute | solution.py:24
  53.1 1.7 collective-permute-done.1
  54.8 0.1 pad_maximum_fusion.18
  55.0 3.0 %collective-permute-start.2 = (bf16[5,18,1,256]{3,2,1,0:T(2,128)(2,1)S(1)}, bf16[5,18,1,256]{3,2,1,0:T(2,128)(2,1)S(1)}, u32[]{:S(2)}, u32[]{:S(2)}) collective-permute-start(bf16[5,18,1,256]{3,2,1,0:T(2,128)(2,1)S(1)} %get-tuple-element.108), channel_id=1, source_target_pairs={{1,0},{2,1},{3,2},{4,3},{5,4},{6,5},{7,6},{8,7},{9,8},{10,9},{11,1... | collective-permute-start | bytes 138248 | tf_op jit(solution)/shard_map/ppermute | solution.py:24
  57.9 1.9 collective-permute-start.3
  59.9 0.0 copy-done.3
  59.9 0.0 copy-done.4
  59.9 0.2 collective-permute-done.2
  60.1 8.5 %collective-permute-done.3 = bf16[5,18,1,256]{3,2,1,0:T(2,128)(2,1)S(1)} collective-permute-done((bf16[5,18,1,256]{3,2,1,0:T(2,128)(2,1)S(1)}, bf16[5,18,1,256]{3,2,1,0:T(2,128)(2,1)S(1)}, u32[]{:S(2)}, u32[]{:S(2)}) %collective-permute-start.3) | collective-permute-done | bytes 46112 | tf_op jit(solution)/shard_map/ppermute | solution.py:22
  68.6 0.0 copy-start
  68.6 5.0 %fusion.27 = bf16[5,16,96,256]{3,2,1,0:T(8,128)(2,1)S(1)} fusion(bf16[5,18,1,256]{3,2,1,0:T(2,128)(2,1)S(1)} %collective-permute-done.3, bf16[5,1,96,256]{3,2,1,0:T(8,128)(2,1)S(1)} %collective-permute-done, bf16[5,16,96,256]{3,2,1,0:T(8,128)(2,1)S(1)} %convolution_convert_fusion, bf16[5,1,96,256]{3,2,1,0:T(8,128)(2,1)S(1)} %collective-permute-done.1, ...), kind=kLoop, calls=%fused_computation.51 | loop fusion | flops 23592960 | bytes 5320704
  73.6 0.0 copy-done
  73.6 2.6 %fusion.30 = bf16[5,16,96,256]{3,2,1,0:T(8,128)(2,1)S(1)} fusion(bf16[5,16,96,256]{3,2,1,0:T(8,128)(2,1)S(1)} %fusion.27, bf16[5,16,96,256]{3,2,1,0:T(8,128)(2,1)S(1)} %convolution_convert_fusion, bf16[5,18,1,256]{3,2,1,0:T(2,128)(2,1)S(1)} %collective-permute-done.3, bf16[5,1,96,256]{3,2,1,0:T(8,128)(2,1)S(1)} %collective-permute-done, ...), kind=kLoop, calls=%fused_computation.54 | loop fusion | flops 20840448 | bytes 7000064
  76.2 5.2 %fusion.31 = bf16[5,16,96,256]{3,2,1,0:T(8,128)(2,1)S(1)} fusion(bf16[5,16,96,256]{3,2,1,0:T(8,128)(2,1)S(1)} %fusion.30, bf16[5,16,96,256]{3,2,1,0:T(8,128)(2,1)S(1)} %convolution_convert_fusion, bf16[5,1,96,256]{3,2,1,0:T(8,128)(2,1)S(1)} %collective-permute-done.1, bf16[5,1,96,256]{3,2,1,0:T(8,128)(2,1)S(1)} %collective-permute-done, ...), kind=kLoop, calls=%fused_computation.55 | loop fusion | flops 22806528 | bytes 6205440
  81.5 2.1 fusion.29
  83.6 5.7 %fusion.28 = bf16[5,16,96,256]{3,2,1,0:T(8,128)(2,1)S(1)} fusion(bf16[5,16,96,256]{3,2,1,0:T(8,128)(2,1)S(1)} %fusion.29, f32[16,96]{1,0:T(8,128)S(1)} %get-tuple-element.115, f32[16,96]{1,0:T(8,128)S(1)} %get-tuple-element.114, f32[16,96]{1,0:T(8,128)S(1)} %get-tuple-element.116, bf16[5,1,96,256]{3,2,1,0:T(8,128)(2,1)S(1)} %collective-permute-done, ...), kind=kLoop, calls=%fused_computation.52 | loop fusion | flops 23592960 | bytes 5419008 | tf_op jit(solution)/shard_map/stack | solution.py:84
  89.3 1.9 fusion.26
  91.2 0.0 reduce-scatter.2.cloned.1.call-update
  91.3 111.7 %reduce-scatter.2.cloned.1.call-done = f32[8,256]{1,0:T(8,128)} async-done(((f32[256,256]{1,0:T(8,128)}), f32[8,256]{1,0:T(8,128)}) %reduce-scatter.2.cloned.1.call-update) | async-done | bytes 8208 | tf_op jit(solution)/shard_map/reduce_scatter | solution.py:106
  202.9 42.1 %all-gather = f32[128,256]{1,0:T(8,128)S(1)} all-gather(f32[8,256]{1,0:T(8,128)} %reduce-scatter.2.cloned.1.call-done), channel_id=2, replica_groups=mesh['sec'=16,'tile'=32] {'sec'}, dimensions={0}, use_global_device_ids=true | all-gather | bytes 139264 | tf_op jit(solution)/shard_map/all_gather | solution.py:33
  245.0 0.5 while.14
  245.5 1.3 add_bitcast_fusion
  (19 shorter events, 0.2 us)
Async XLA Ops:
  6.5 196.4 %reduce-scatter.2.cloned.1.call-start = ((), (), s32[]{:S(2)}) async-start(), calls=%async_computation.2 | async-start | bytes 270336 | tf_op jit(solution)/shard_map/reduce_scatter | solution.py:106
  39.6 9.3 %copy-start.1 = (f32[16,96]{1,0:T(8,128)S(1)}, f32[16,96]{1,0:T(8,128)}, u32[]{:S(2)}) copy-start(f32[16,96]{1,0:T(8,128)} %param.13) | copy-start | bytes 18436
  39.6 9.3 %copy-start.2 = (f32[16,96]{1,0:T(8,128)S(1)}, f32[16,96]{1,0:T(8,128)}, u32[]{:S(2)}) copy-start(f32[16,96]{1,0:T(8,128)} %param.12) | copy-start | bytes 18436
  43.0 10.0 %collective-permute-start = (bf16[5,1,96,256]{3,2,1,0:T(8,128)(2,1)S(1)}, bf16[5,1,96,256]{3,2,1,0:T(8,128)(2,1)S(1)}, u32[]{:S(2)}, u32[]{:S(2)}) collective-permute-start(bf16[5,1,96,256]{3,2,1,0:T(8,128)(2,1)S(1)} %get-tuple-element.111), channel_id=1, source_target_pairs={{32,0},{64,32},{96,64},{128,96},{160,128},{192,160},{224,192},{256... | collective-permute-start | bytes 737288 | tf_op jit(solution)/shard_map/ppermute | solution.py:24
  44.3 10.5 %collective-permute-start.1 = (bf16[5,1,96,256]{3,2,1,0:T(8,128)(2,1)S(1)}, bf16[5,1,96,256]{3,2,1,0:T(8,128)(2,1)S(1)}, u32[]{:S(2)}, u32[]{:S(2)}) collective-permute-start(bf16[5,1,96,256]{3,2,1,0:T(8,128)(2,1)S(1)} %get-tuple-element.110), channel_id=1, source_target_pairs={{0,32},{32,64},{64,96},{96,128},{128,160},{160,192},{192,224},{224... | collective-permute-start | bytes 737288 | tf_op jit(solution)/shard_map/ppermute | solution.py:22
  49.0 10.9 %copy-start.3 = (f32[16,96]{1,0:T(8,128)S(1)}, f32[16,96]{1,0:T(8,128)}, u32[]{:S(2)}) copy-start(f32[16,96]{1,0:T(8,128)} %param.15) | copy-start | bytes 18436
  49.0 10.9 %copy-start.4 = (f32[16,96]{1,0:T(8,128)S(1)}, f32[16,96]{1,0:T(8,128)}, u32[]{:S(2)}) copy-start(f32[16,96]{1,0:T(8,128)} %param.11) | copy-start | bytes 18436
  55.0 5.1 %collective-permute-start.2 = (bf16[5,18,1,256]{3,2,1,0:T(2,128)(2,1)S(1)}, bf16[5,18,1,256]{3,2,1,0:T(2,128)(2,1)S(1)}, u32[]{:S(2)}, u32[]{:S(2)}) collective-permute-start(bf16[5,18,1,256]{3,2,1,0:T(2,128)(2,1)S(1)} %get-tuple-element.108), channel_id=1, source_target_pairs={{1,0},{2,1},{3,2},{4,3},{5,4},{6,5},{7,6},{8,7},{9,8},{10,9},{11,1... | collective-permute-start | bytes 138248 | tf_op jit(solution)/shard_map/ppermute | solution.py:24
  57.9 10.7 %collective-permute-start.3 = (bf16[5,18,1,256]{3,2,1,0:T(2,128)(2,1)S(1)}, bf16[5,18,1,256]{3,2,1,0:T(2,128)(2,1)S(1)}, u32[]{:S(2)}, u32[]{:S(2)}) collective-permute-start(bf16[5,18,1,256]{3,2,1,0:T(2,128)(2,1)S(1)} %get-tuple-element.109), channel_id=1, source_target_pairs={{0,1},{1,2},{2,3},{3,4},{4,5},{5,6},{6,7},{7,8},{8,9},{9,10},{10,1... | collective-permute-start | bytes 138248 | tf_op jit(solution)/shard_map/ppermute | solution.py:22
  68.6 5.0 %copy-start = (f32[16,96]{1,0:T(8,128)S(1)}, f32[16,96]{1,0:T(8,128)}, u32[]{:S(2)}) copy-start(f32[16,96]{1,0:T(8,128)} %param.14) | copy-start | bytes 18436
Sparse Core Ops, SparseCore 0:
  91.4 111.5 reduce-scatter.1
